TPU v7x, 32 devices: a whole 2x2x4 slice. The times are simulated.
32 devices in a mesh: group: 2 (over y), phi: 4 (over z), eta: 2 (over x), half: 2 (over core).
Axes of the slice: x: 2, y: 2, z: 4, core: 2. Of those that a mesh axis runs over, the one named last changes fastest.
Arguments:
- feats: bfloat16 [8, 2, 512, 512], P(('group', 'phi'), 'eta', 'half'), parts along dimension 0, may hold values from -6 to 6
- cotangent: bfloat16 [8, 2, 512, 512], P(('group', 'phi'), 'eta', 'half'), parts along dimension 0, may hold values from -6 to 6
- tiles: bfloat16 [8, 2, 24, 128, 128], P(('group', 'phi'), 'eta', 'half'), parts along dimension 0, may hold values from -0.21875 to 0.21875
- tile_src: int32 [8, 2, 24], P(('group', 'phi'), 'eta', 'half'), parts along dimension 0, may hold values from 0 to 5
- tile_dst: int32 [8, 2, 24], P(('group', 'phi'), 'eta', 'half'), parts along dimension 0, may hold values from -1 to 3, as said below
- weights: bfloat16 [2, 512, 512], replicated, may hold values from -0.25 to 0.25
- mask: int32 [2, 8, 8], replicated, may hold values 0 or 1
- counts: int32 [8, 2], P(('group', 'phi'), 'eta'), parts along dimension 0, may hold values from 128 to 512, as said below
Outputs:
- final: bfloat16 [8, 2, 512, 512], P(('group', 'phi'), 'eta', 'half'), parts along dimension 0
- grad_w: float32 [4, 512, 512], P('group', 'phi'), parts along dimension 0
There are 2 independent parts, one for each index of `group`. A program takes and returns all parts, laid end to end along the dimension named above; an argument that names none is the same for every part. Nothing has to cross between parts.
Inputs may be any that keep to these rules, and one draw needn't show every extreme that they name: `tile_dst`: in each region half the live tiles fill the first slots and the rest hold -1; some region half has all 12 slots live. `counts`: some region is full and some holds a quarter of its hits.
All inputs are finite; a program needn't handle non-finite values.
Results may differ from a plain program's by a relative error of at most 0.017.
Values may be sent and summed in bfloat16 or wider, within the bound.
No kernel may reach another device: no remote copies, remote signals or barrier semaphores. Data moves between devices by JAX's collectives and lax.ppermute only.
A program may use at most 64 MiB of HBM per device.

v0:
```python
import jax
import jax.numpy as jnp
from jax import lax
from jax.sharding import PartitionSpec as P


def with_halo(block, sides, width, periodic):
    for axis, dim in sides:
        count = lax.axis_size(axis)
        forward = [(i, i + 1) for i in range(count - 1)]
        if periodic:
            forward.append((count - 1, 0))
        backward = [(target, source) for source, target in forward]
        low = lax.ppermute(
            lax.slice_in_dim(block, block.shape[dim] - width, None, axis=dim), axis, forward
        )
        high = lax.ppermute(lax.slice_in_dim(block, 0, width, axis=dim), axis, backward)
        block = jnp.concatenate([low, block, high], axis=dim)
    return block


def silu_slope(pre):
    sigma = jax.nn.sigmoid(pre)
    return sigma * (1.0 + pre * (1.0 - sigma))


def body(feats, cotangent, tiles, tile_src, tile_dst, weights, mask, counts):
    rows = feats.shape[2]
    width = feats.shape[3]
    block = tiles.shape[3]
    own_blocks = rows // block
    halves = lax.axis_size("half")
    region_blocks = own_blocks * halves
    slots = own_blocks + 4
    layers = weights.shape[0]
    grid = mask.shape[1]
    side = width // grid
    tile_set = tiles[0, 0]
    sources_of = tile_src[0, 0]
    targets = tile_dst[0, 0]
    first_row = lax.axis_index("half") * rows
    live = (first_row + jnp.arange(rows, dtype=jnp.int32) < counts[0, 0]).astype(jnp.float32)[
        :, None
    ]
    eta_here = lax.axis_index("eta")
    lower_eta = (eta_here > 0).astype(jnp.bfloat16)
    upper_eta = (eta_here < lax.axis_size("eta") - 1).astype(jnp.bfloat16)
    mask_full = (
        jnp.broadcast_to(mask[:, :, None, :, None], (layers, grid, side, grid, side))
        .reshape(layers, width, width)
        .astype(jnp.float32)
    )
    masked = (weights.astype(jnp.float32) * mask_full).astype(jnp.bfloat16)
    block_ids = jnp.arange(region_blocks, dtype=jnp.int32)
    slot_ids = jnp.arange(slots, dtype=jnp.int32)
    state = feats[0, 0]
    inputs = []
    pres = []
    for layer in range(layers):
        edge = state[:block][None, None]
        padded = with_halo(edge, (("phi", 0), ("eta", 1)), 1, True)
        rims = jnp.stack(
            [padded[0, 1], padded[2, 1], padded[1, 0] * lower_eta, padded[1, 2] * upper_eta]
        )
        messages_picked = jnp.take(
            jnp.concatenate([state.reshape(own_blocks, block, width), rims], axis=0),
            sources_of,
            axis=0,
        )
        messages_parts = jnp.einsum(
            "tij,tjd->tid", tile_set, messages_picked, preferred_element_type=jnp.float32
        )
        messages_onehot = (targets[None, :] == block_ids[:, None]).astype(jnp.float32)
        messages_total = jnp.einsum(
            "bt,tid->bid", messages_onehot, messages_parts, precision=lax.Precision.HIGHEST
        )
        region = messages_total.reshape(region_blocks * block, width)
        gathered = lax.psum_scatter(
            region.astype(jnp.bfloat16), "half", scatter_dimension=0, tiled=True
        ).astype(jnp.float32)
        hfloat = state.astype(jnp.float32)
        mixed = (hfloat + gathered).astype(jnp.bfloat16)
        pre = jnp.dot(mixed, masked[layer], preferred_element_type=jnp.float32)
        state = (live * (hfloat + jax.nn.silu(pre))).astype(jnp.bfloat16)
        inputs.append(mixed)
        pres.append(pre)
    upstream = cotangent[0, 0].astype(jnp.float32)
    partials = [None] * layers
    for layer in reversed(range(layers)):
        delta = (upstream * live * silu_slope(pres[layer])).astype(jnp.bfloat16)
        partials[layer] = (
            jnp.einsum("rd,re->de", inputs[layer], delta, preferred_element_type=jnp.float32)
            * mask_full[layer]
        )
        if layer > 0:
            back = jnp.einsum(
                "re,de->rd", delta, masked[layer], preferred_element_type=jnp.float32
            ).astype(jnp.bfloat16)
            whole = lax.all_gather(back, "half", axis=0, tiled=True)
            valid = (targets >= 0).astype(jnp.bfloat16)
            picked = (
                jnp.take(
                    whole.reshape(region_blocks, block, width), jnp.maximum(targets, 0), axis=0
                )
                * valid[:, None, None]
            )
            parts = jnp.einsum("tji,tjd->tid", tile_set, picked, preferred_element_type=jnp.float32)
            onehot = (sources_of[None, :] == slot_ids[:, None]).astype(jnp.float32)
            total = jnp.einsum("st,tid->sid", onehot, parts, precision=lax.Precision.HIGHEST)
            returned_phi = with_halo(
                total[own_blocks : own_blocks + 2].astype(jnp.bfloat16), (("phi", 0),), 1, True
            ).astype(jnp.float32)
            returned_eta = with_halo(
                total[own_blocks + 2 :].astype(jnp.bfloat16), (("eta", 0),), 1, False
            ).astype(jnp.float32)
            extra = returned_phi[0] + returned_phi[3] + returned_eta[0] + returned_eta[3]
            own = total[:own_blocks].reshape(rows, width)
            own = jnp.concatenate([own[:block] + extra, own[block:]], axis=0)
            upstream = live * upstream + back.astype(jnp.float32) + own
    stacked = jnp.stack(partials)
    shares = lax.psum_scatter(stacked.astype(jnp.bfloat16), "phi", scatter_dimension=1, tiled=True)
    result = lax.psum(shares, ("eta", "half")).astype(jnp.float32)
    return (state[None, None], result)


def solution(mesh):
    in_specs = (
        P(("group", "phi"), "eta", "half", None),
        P(("group", "phi"), "eta", "half", None),
        P(("group", "phi"), "eta", "half", None, None),
        P(("group", "phi"), "eta", "half"),
        P(("group", "phi"), "eta", "half"),
        P(),
        P(),
        P(("group", "phi"), "eta"),
    )
    out_specs = (P(("group", "phi"), "eta", "half", None), P("group", "phi", None))
    return jax.shard_map(body, mesh=mesh, in_specs=in_specs, out_specs=out_specs, check_vma=False)
```

profile of v0, /device:TPU:0, one launch (start us, length us, event | category | flops | bytes accessed | tf_op | source)
XLA Modules:
  0.0 213.0 jit_solution(10340029275667400948)
XLA Ops:
  8.2 3.1 %collective-permute-start = (bf16[1,1,128,512]{3,2,1,0:T(8,128)(2,1)S(1)}, bf16[1,1,128,512]{3,2,1,0:T(8,128)(2,1)S(1)}, u32[]{:S(2)}, u32[]{:S(2)}) collective-permute-start(bf16[1,1,128,512]{3,2,1,0:T(8,128)(2,1)S(1)} %slice.89), channel_id=1, source_target_pairs={{0,4},{4,8},{8,12},{12,0},{1,5},{5,9},{9,13},{13,1},{2,6},{6,10},{... | collective-permute-start | bytes 393224 | tf_op jit(solution)/shard_map/ppermute | solution.py:14
  21.2 10.0 %collective-permute-done.2 = bf16[3,1,128,512]{3,2,1,0:T(8,128)(2,1)S(1)} collective-permute-done((bf16[3,1,128,512]{3,2,1,0:T(8,128)(2,1)S(1)}, bf16[3,1,128,512]{3,2,1,0:T(8,128)(2,1)S(1)}, u32[]{:S(2)}, u32[]{:S(2)}) %collective-permute-start.2) | collective-permute-done | bytes 393248 | tf_op jit(solution)/shard_map/ppermute | solution.py:14
  31.2 6.8 %collective-permute-done.3 = bf16[3,1,128,512]{3,2,1,0:T(8,128)(2,1)S(1)} collective-permute-done((bf16[3,1,128,512]{3,2,1,0:T(8,128)(2,1)S(1)}, bf16[3,1,128,512]{3,2,1,0:T(8,128)(2,1)S(1)}, u32[]{:S(2)}, u32[]{:S(2)}) %collective-permute-start.3) | collective-permute-done | bytes 393248 | tf_op jit(solution)/shard_map/ppermute | solution.py:17
  42.0 3.5 %copy.19 = f32[12,512,128]{1,0,2:T(8,128)} copy(f32[12,512,128]{2,1,0:T(8,128)S(1)} %fusion.8) | data formatting | bytes 6291456 | tf_op jit(solution)/shard_map/tij,tjd->tid/dot_general | solution.py:70
  45.5 3.8 %fusion.16 = bf16[4,128,512]{2,0,1:T(4,128)(2,1)S(1)} fusion(f32[12,512,128]{1,0,2:T(8,128)} %copy.19, s32[12]{0:T(128)S(1)} %bitcast.122), kind=kOutput, calls=%fused_computation.22 | convolution fusion | flops 38010928 | bytes 3670064 | tf_op jit(solution)/shard_map/bt,tid->bid/dot_general | solution.py:74
  50.3 2.3 %broadcast_in_dim.41 = f32[2,8,64,8,64]{4,3,2,1,0:T(8,128)} broadcast(f32[2,8,8]{2,1,0:T(8,128)S(1)} %convert_element_type.115), dimensions={0,1,3} | broadcast | bytes 2097664 | tf_op jit(solution)/shard_map/broadcast_in_dim | solution.py:49
  52.6 3.5 %convert_element_type.116 = f32[2,512,512]{2,1,0:T(8,128)S(1)} reshape(f32[2,8,64,8,64]{4,3,2,1,0:T(8,128)} %broadcast_in_dim.41) | data formatting | bytes 4194304 | tf_op jit(solution)/shard_map/convert_element_type | solution.py:51
  58.7 2.4 %fusion.35 = (bf16[256,512]{1,0:T(8,128)(2,1)S(1)}, f32[256,512]{1,0:T(8,128)}) fusion(bf16[1,1,256,512]{3,2,1,0:T(8,128)(2,1)} %param.10, f32[256]{0:T(256)} %compare_convert_fusion.1, bf16[2,512,512]{2,1,0:T(8,128)(2,1)} %multiply_convert_fusion, bf16[256,512]{1,0:T(8,128)(2,1)} %reduce-scatter.4.cloned.1.call-done), kind=kOutput, calls=%fused_computation.43 | convolution fusion | flops 135790592 | bytes 2098176 | tf_op jit(solution)/shard_map/dot_general | solution.py:83
  65.0 4.4 %collective-permute-done.4 = bf16[1,1,128,512]{3,2,1,0:T(8,128)(2,1)S(1)} collective-permute-done((bf16[1,1,128,512]{3,2,1,0:T(8,128)(2,1)S(1)}, bf16[1,1,128,512]{3,2,1,0:T(8,128)(2,1)S(1)}, u32[]{:S(2)}, u32[]{:S(2)}) %collective-permute-start.4) | collective-permute-done | bytes 131104 | tf_op jit(solution)/shard_map/ppermute | solution.py:14
  72.6 10.0 %collective-permute-done.6 = bf16[3,1,128,512]{3,2,1,0:T(8,128)(2,1)S(1)} collective-permute-done((bf16[3,1,128,512]{3,2,1,0:T(8,128)(2,1)S(1)}, bf16[3,1,128,512]{3,2,1,0:T(8,128)(2,1)S(1)}, u32[]{:S(2)}, u32[]{:S(2)}) %collective-permute-start.6) | collective-permute-done | bytes 393248 | tf_op jit(solution)/shard_map/ppermute | solution.py:14
  82.7 6.9 %collective-permute-done.7 = bf16[3,1,128,512]{3,2,1,0:T(8,128)(2,1)S(1)} collective-permute-done((bf16[3,1,128,512]{3,2,1,0:T(8,128)(2,1)S(1)}, bf16[3,1,128,512]{3,2,1,0:T(8,128)(2,1)S(1)}, u32[]{:S(2)}, u32[]{:S(2)}) %collective-permute-start.7) | collective-permute-done | bytes 393248 | tf_op jit(solution)/shard_map/ppermute | solution.py:17
  93.6 3.5 %copy.20 = f32[12,512,128]{1,0,2:T(8,128)} copy(f32[12,512,128]{2,1,0:T(8,128)S(1)} %fusion.6) | data formatting | bytes 6291456 | tf_op jit(solution)/shard_map/tij,tjd->tid/dot_general | solution.py:70
  97.1 3.8 %fusion.19 = bf16[4,128,512]{2,0,1:T(4,128)(2,1)S(1)} fusion(f32[12,512,128]{1,0,2:T(8,128)} %copy.20, s32[12]{0:T(128)S(1)} %bitcast.123), kind=kOutput, calls=%fused_computation.23 | convolution fusion | flops 38010928 | bytes 3670064 | tf_op jit(solution)/shard_map/bt,tid->bid/dot_general | solution.py:74
  105.3 4.0 %reduce-scatter.6.cloned.1.call-done = bf16[256,512]{1,0:T(8,128)(2,1)} async-done(((bf16[512,512]{1,0:T(8,128)(2,1)}), bf16[256,512]{1,0:T(8,128)(2,1)}) %reduce-scatter.6.cloned.1.call-update) | async-done | bytes 262160 | tf_op jit(solution)/shard_map/reduce_scatter | solution.py:78
  109.3 2.4 %fusion.42 = (bf16[256,512]{1,0:T(8,128)(2,1)S(1)}, bf16[1,1,256,512]{3,2,1,0:T(8,128)(2,1)}) fusion(bf16[1,1,256,512]{3,2,1,0:T(8,128)(2,1)S(1)} %copy-done.19, f32[256]{0:T(256)S(1)} %copy-done.17, bf16[256,512]{1,0:T(8,128)(2,1)S(1)} %copy-done.3, bf16[2,512,512]{2,1,0:T(8,128)(2,1)} %multiply_convert_fusion, ...), kind=kOutput, calls=%fused_computation.54 | convolution fusion | flops 136839168 | bytes 2098176 | tf_op jit(solution)/shard_map/dot_general | solution.py:83
  112.7 2.3 %all_gather.3 = bf16[512,512]{1,0:T(8,128)(2,1)S(1)} all-gather(bf16[256,512]{1,0:T(8,128)(2,1)S(1)} %convolution_convert_fusion), channel_id=1, replica_groups=mesh['group'=2,'phi'=4,'eta'=2,'half'=2] {'half'}, dimensions={0}, use_global_device_ids=true | all-gather | bytes 786432 | tf_op jit(solution)/shard_map/all_gather | solution.py:99
  116.9 2.1 %fusion.10 = f32[12,512,128]{2,1,0:T(8,128)S(1)} fusion(bf16[12,128,512]{2,1,0:T(8,128)(2,1)} %gather_fusion, pred[12]{0:T(512)(128)(4,1)S(1)} %get-tuple-element.18, bf16[12]{0:T(256)(128)(2,1)S(1)} %get-tuple-element.17, bf16[1,1,12,128,128]{4,3,2,1,0:T(8,128)(2,1)S(1)} %copy-done), kind=kOutput, calls=%fused_computation.14 | convolution fusion | flops 202899456 | bytes 5111844 | tf_op jit(solution)/shard_map/tji,tjd->tid/dot_general | solution.py:107
  119.1 3.5 %copy.21 = f32[12,512,128]{1,0,2:T(8,128)} copy(f32[12,512,128]{2,1,0:T(8,128)S(1)} %fusion.10) | data formatting | bytes 6291456 | tf_op jit(solution)/shard_map/tji,tjd->tid/dot_general | solution.py:107
  122.6 3.7 %fusion = f32[6,128,512]{2,0,1:T(8,128)S(1)} fusion(f32[12,512,128]{1,0,2:T(8,128)} %copy.21, s32[12]{0:T(128)S(1)} %bitcast.124), kind=kOutput, calls=%fused_computation.3 | convolution fusion | flops 56623176 | bytes 4718640 | tf_op jit(solution)/shard_map/st,tid->sid/dot_general | solution.py:109
  127.4 3.8 %collective-permute-start.10 = (bf16[1,128,512]{2,1,0:T(8,128)(2,1)S(1)}, bf16[1,128,512]{2,1,0:T(8,128)(2,1)S(1)}, u32[]{:S(2)}, u32[]{:S(2)}) collective-permute-start(bf16[1,128,512]{2,1,0:T(8,128)(2,1)S(1)} %get-tuple-element.9), channel_id=1, source_target_pairs={{0,2},{1,3},{4,6},{5,7},{8,10},{9,11},{12,14},{13,15},{16,18},{17,... | collective-permute-start | bytes 393224 | tf_op jit(solution)/shard_map/ppermute | solution.py:14
  134.0 2.3 %collective-permute-start.9 = (bf16[1,128,512]{2,1,0:T(8,128)(2,1)S(1)}, bf16[1,128,512]{2,1,0:T(8,128)(2,1)S(1)}, u32[]{:S(2)}, u32[]{:S(2)}) collective-permute-start(bf16[1,128,512]{2,1,0:T(8,128)(2,1)S(1)} %get-tuple-element.10), channel_id=1, source_target_pairs={{4,0},{8,4},{12,8},{0,12},{5,1},{9,5},{13,9},{1,13},{6,2},{10,6},{... | collective-permute-start | bytes 393224 | tf_op jit(solution)/shard_map/ppermute | solution.py:17
  138.5 2.2 %collective-permute-done.8 = bf16[1,128,512]{2,1,0:T(8,128)(2,1)S(1)} collective-permute-done((bf16[1,128,512]{2,1,0:T(8,128)(2,1)S(1)}, bf16[1,128,512]{2,1,0:T(8,128)(2,1)S(1)}, u32[]{:S(2)}, u32[]{:S(2)}) %collective-permute-start.8) | collective-permute-done | bytes 131104 | tf_op jit(solution)/shard_map/ppermute | solution.py:14
  143.9 27.9 %reduce-scatter.8.cloned.1.call-done = bf16[2,128,512]{2,1,0:T(8,128)(2,1)} async-done(((bf16[2,512,512]{2,1,0:T(8,128)(2,1)}), bf16[2,128,512]{2,1,0:T(8,128)(2,1)}) %reduce-scatter.8.cloned.1.call-update) | async-done | bytes 262160 | tf_op jit(solution)/shard_map/reduce_scatter | solution.py:121
  171.8 32.9 %all-reduce.2.cloned.1.call-done = bf16[2,128,512]{2,1,0:T(8,128)(2,1)} async-done(((bf16[2,128,512]{2,1,0:T(8,128)(2,1)}), bf16[2,128,512]{2,1,0:T(8,128)(2,1)}) %all-reduce.2.cloned.1.call-update) | async-done | bytes 262160 | tf_op jit(solution)/shard_map/psum | solution.py:122
  (114 shorter events, 47.2 us)
Async XLA Ops:
  7.2 32.7 %copy-start = (bf16[1,1,12,128,128]{4,3,2,1,0:T(8,128)(2,1)S(1)}, bf16[1,1,12,128,128]{4,3,2,1,0:T(8,128)(2,1)}, u32[]{:S(2)}) copy-start(bf16[1,1,12,128,128]{4,3,2,1,0:T(8,128)(2,1)} %param.12) | copy-start | bytes 1179652
  7.2 51.5 %reduce-scatter.4.cloned.1.call-start = ((), (), s32[]{:S(2)}) async-start(), calls=%async_computation.3 | async-start | bytes 786432 | tf_op jit(solution)/shard_map/reduce_scatter | solution.py:78
  8.2 9.4 %collective-permute-start = (bf16[1,1,128,512]{3,2,1,0:T(8,128)(2,1)S(1)}, bf16[1,1,128,512]{3,2,1,0:T(8,128)(2,1)S(1)}, u32[]{:S(2)}, u32[]{:S(2)}) collective-permute-start(bf16[1,1,128,512]{3,2,1,0:T(8,128)(2,1)S(1)} %slice.89), channel_id=1, source_target_pairs={{0,4},{4,8},{8,12},{12,0},{1,5},{5,9},{9,13},{13,1},{2,6},{6,10},{... | collective-permute-start | bytes 393224 | tf_op jit(solution)/shard_map/ppermute | solution.py:14
  11.3 7.8 %collective-permute-start.1 = (bf16[1,1,128,512]{3,2,1,0:T(8,128)(2,1)S(1)}, bf16[1,1,128,512]{3,2,1,0:T(8,128)(2,1)S(1)}, u32[]{:S(2)}, u32[]{:S(2)}) collective-permute-start(bf16[1,1,128,512]{3,2,1,0:T(8,128)(2,1)S(1)} %slice.89), channel_id=1, source_target_pairs={{4,0},{8,4},{12,8},{0,12},{5,1},{9,5},{13,9},{1,13},{6,2},{10,6},{... | collective-permute-start | bytes 393224 | tf_op jit(solution)/shard_map/ppermute | solution.py:17
  14.7 25.2 %copy-start.16 = (pred[12]{0:T(512)(128)(4,1)}, pred[12]{0:T(512)(128)(4,1)S(1)}, u32[]{:S(2)}) copy-start(pred[12]{0:T(512)(128)(4,1)S(1)} %compare_and_fusion) | copy-start | bytes 40
  19.1 12.1 %collective-permute-start.2 = (bf16[3,1,128,512]{3,2,1,0:T(8,128)(2,1)S(1)}, bf16[3,1,128,512]{3,2,1,0:T(8,128)(2,1)S(1)}, u32[]{:S(2)}, u32[]{:S(2)}) collective-permute-start(bf16[3,1,128,512]{3,2,1,0:T(8,128)(2,1)S(1)} %pad_maximum_fusion.1), channel_id=1, source_target_pairs={{0,2},{2,0},{1,3},{3,1},{4,6},{6,4},{5,7},{7,5},{8,10},{10,8},{9,1... | collective-permute-start | bytes 1179656 | tf_op jit(solution)/shard_map/ppermute | solution.py:14
  20.6 17.4 %collective-permute-start.3 = (bf16[3,1,128,512]{3,2,1,0:T(8,128)(2,1)S(1)}, bf16[3,1,128,512]{3,2,1,0:T(8,128)(2,1)S(1)}, u32[]{:S(2)}, u32[]{:S(2)}) collective-permute-start(bf16[3,1,128,512]{3,2,1,0:T(8,128)(2,1)S(1)} %pad_maximum_fusion.1), channel_id=1, source_target_pairs={{2,0},{0,2},{3,1},{1,3},{6,4},{4,6},{7,5},{5,7},{10,8},{8,10},{11,... | collective-permute-start | bytes 1179656 | tf_op jit(solution)/shard_map/ppermute | solution.py:17
  50.2 59.1 %reduce-scatter.6.cloned.1.call-start = ((), (), s32[]{:S(2)}) async-start(), calls=%async_computation.4 | async-start | bytes 786432 | tf_op jit(solution)/shard_map/reduce_scatter | solution.py:78
  61.1 21.6 %copy-start.2 = (bf16[256,512]{1,0:T(8,128)(2,1)}, bf16[256,512]{1,0:T(8,128)(2,1)S(1)}, u32[]{:S(2)}) copy-start(bf16[256,512]{1,0:T(8,128)(2,1)S(1)} %get-tuple-element.19) | copy-start | bytes 786436
  61.1 8.3 %collective-permute-start.4 = (bf16[1,1,128,512]{3,2,1,0:T(8,128)(2,1)S(1)}, bf16[1,1,128,512]{3,2,1,0:T(8,128)(2,1)S(1)}, u32[]{:S(2)}, u32[]{:S(2)}) collective-permute-start(bf16[1,1,128,512]{3,2,1,0:T(8,128)(2,1)S(1)} %slice_bitcast_fusion.6), channel_id=1, source_target_pairs={{0,4},{4,8},{8,12},{12,0},{1,5},{5,9},{9,13},{13,1},{2,6},{6,10},{... | collective-permute-start | bytes 393224 | tf_op jit(solution)/shard_map/ppermute | solution.py:14
  62.9 7.6 %collective-permute-start.5 = (bf16[1,1,128,512]{3,2,1,0:T(8,128)(2,1)S(1)}, bf16[1,1,128,512]{3,2,1,0:T(8,128)(2,1)S(1)}, u32[]{:S(2)}, u32[]{:S(2)}) collective-permute-start(bf16[1,1,128,512]{3,2,1,0:T(8,128)(2,1)S(1)} %slice_bitcast_fusion.6), channel_id=1, source_target_pairs={{4,0},{8,4},{12,8},{0,12},{5,1},{9,5},{13,9},{1,13},{6,2},{10,6},{... | collective-permute-start | bytes 393224 | tf_op jit(solution)/shard_map/ppermute | solution.py:17
  70.5 12.1 %collective-permute-start.6 = (bf16[3,1,128,512]{3,2,1,0:T(8,128)(2,1)S(1)}, bf16[3,1,128,512]{3,2,1,0:T(8,128)(2,1)S(1)}, u32[]{:S(2)}, u32[]{:S(2)}) collective-permute-start(bf16[3,1,128,512]{3,2,1,0:T(8,128)(2,1)S(1)} %pad_maximum_fusion.2), channel_id=1, source_target_pairs={{0,2},{2,0},{1,3},{3,1},{4,6},{6,4},{5,7},{7,5},{8,10},{10,8},{9,1... | collective-permute-start | bytes 1179656 | tf_op jit(solution)/shard_map/ppermute | solution.py:14
  72.0 17.5 %collective-permute-start.7 = (bf16[3,1,128,512]{3,2,1,0:T(8,128)(2,1)S(1)}, bf16[3,1,128,512]{3,2,1,0:T(8,128)(2,1)S(1)}, u32[]{:S(2)}, u32[]{:S(2)}) collective-permute-start(bf16[3,1,128,512]{3,2,1,0:T(8,128)(2,1)S(1)} %pad_maximum_fusion.2), channel_id=1, source_target_pairs={{2,0},{0,2},{3,1},{1,3},{6,4},{4,6},{7,5},{5,7},{10,8},{8,10},{11,... | collective-permute-start | bytes 1179656 | tf_op jit(solution)/shard_map/ppermute | solution.py:17
  101.8 70.0 %reduce-scatter.8.cloned.1.call-start = ((), (), s32[]{:S(2)}) async-start(), calls=%async_computation.5 | async-start | bytes 1310720 | tf_op jit(solution)/shard_map/reduce_scatter | solution.py:121
  105.2 6.4 %copy-start.7 = (bf16[2,512,512]{2,1,0:T(8,128)(2,1)S(1)}, bf16[2,512,512]{2,1,0:T(8,128)(2,1)}, u32[]{:S(2)}) copy-start(bf16[2,512,512]{2,1,0:T(8,128)(2,1)} %multiply_convert_fusion) | copy-start | bytes 3145732
  127.3 9.1 %copy-start.1 = (f32[512,512]{1,0:T(8,128)S(1)}, f32[512,512]{1,0:T(8,128)}, u32[]{:S(2)}) copy-start(f32[512,512]{1,0:T(8,128)} %squeeze.39) | copy-start | bytes 3145732
  127.3 9.1 %copy-start.4 = (bf16[256,512]{1,0:T(8,128)(2,1)S(1)}, bf16[256,512]{1,0:T(8,128)(2,1)}, u32[]{:S(2)}) copy-start(bf16[256,512]{1,0:T(8,128)(2,1)} %copy-done.2) | copy-start | bytes 786436
  127.3 9.1 %copy-start.11 = (bf16[256,512]{1,0:T(8,128)(2,1)S(1)}, bf16[256,512]{1,0:T(8,128)(2,1)}, u32[]{:S(2)}) copy-start(bf16[256,512]{1,0:T(8,128)(2,1)} %reduce-scatter.6.cloned.1.call-done) | copy-start | bytes 786436
  127.3 9.0 %copy-start.13 = (bf16[256,512]{1,0:T(8,128)(2,1)S(1)}, bf16[256,512]{1,0:T(8,128)(2,1)}, u32[]{:S(2)}) copy-start(bf16[256,512]{1,0:T(8,128)(2,1)} %copy-done.12) | copy-start | bytes 786436
  127.4 9.4 %collective-permute-start.10 = (bf16[1,128,512]{2,1,0:T(8,128)(2,1)S(1)}, bf16[1,128,512]{2,1,0:T(8,128)(2,1)S(1)}, u32[]{:S(2)}, u32[]{:S(2)}) collective-permute-start(bf16[1,128,512]{2,1,0:T(8,128)(2,1)S(1)} %get-tuple-element.9), channel_id=1, source_target_pairs={{0,2},{1,3},{4,6},{5,7},{8,10},{9,11},{12,14},{13,15},{16,18},{17,... | collective-permute-start | bytes 393224 | tf_op jit(solution)/shard_map/ppermute | solution.py:14
  131.1 7.3 %collective-permute-start.11 = (bf16[1,128,512]{2,1,0:T(8,128)(2,1)S(1)}, bf16[1,128,512]{2,1,0:T(8,128)(2,1)S(1)}, u32[]{:S(2)}, u32[]{:S(2)}) collective-permute-start(bf16[1,128,512]{2,1,0:T(8,128)(2,1)S(1)} %get-tuple-element.8), channel_id=1, source_target_pairs={{2,0},{3,1},{6,4},{7,5},{10,8},{11,9},{14,12},{15,13},{18,16},{19,... | collective-permute-start | bytes 393224 | tf_op jit(solution)/shard_map/ppermute | solution.py:17
  132.4 8.2 %collective-permute-start.8 = (bf16[1,128,512]{2,1,0:T(8,128)(2,1)S(1)}, bf16[1,128,512]{2,1,0:T(8,128)(2,1)S(1)}, u32[]{:S(2)}, u32[]{:S(2)}) collective-permute-start(bf16[1,128,512]{2,1,0:T(8,128)(2,1)S(1)} %get-tuple-element.7), channel_id=1, source_target_pairs={{0,4},{4,8},{8,12},{12,0},{1,5},{5,9},{9,13},{13,1},{2,6},{6,10},{... | collective-permute-start | bytes 393224 | tf_op jit(solution)/shard_map/ppermute | solution.py:14
  134.0 8.0 %collective-permute-start.9 = (bf16[1,128,512]{2,1,0:T(8,128)(2,1)S(1)}, bf16[1,128,512]{2,1,0:T(8,128)(2,1)S(1)}, u32[]{:S(2)}, u32[]{:S(2)}) collective-permute-start(bf16[1,128,512]{2,1,0:T(8,128)(2,1)S(1)} %get-tuple-element.10), channel_id=1, source_target_pairs={{4,0},{8,4},{12,8},{0,12},{5,1},{9,5},{13,9},{1,13},{6,2},{10,6},{... | collective-permute-start | bytes 393224 | tf_op jit(solution)/shard_map/ppermute | solution.py:17
  143.8 60.8 %all-reduce.2.cloned.1.call-start = ((), (), s32[]{:S(2)}) async-start(), calls=%async_computation.6 | async-start | bytes 524288 | tf_op jit(solution)/shard_map/psum | solution.py:122
  (15 other events, 68.0 us)
Sparse Core Ops, SparseCore 0:
  50.3 7.6 reduce-scatter.3
  101.9 7.3 reduce-scatter.5
  143.9 27.7 reduce-scatter.7
  174.0 30.5 all-reduce.1
where the time goes:
time: 214 us; the launch traced here: 213 us
  waiting for transfers between devices  113 us (53%)
  local copies, waits for them, and re-layouts  29.8 us (14%)
  matrix products  23.7 us (11%)
  starting transfers between devices  22.3 us (10%)
  between operations  14.9 us (7%)
  other arithmetic  7.39 us (3%)
  blocking collectives  2.35 us (1%)
    psum x1, waiting for transfers between devices, body(): result = lax.psum(shares, ('eta', 'half')).astype(jnp.float32)  32.9 us
    ppermute x6, waiting for transfers between devices, with_halo(): lax.ppermute(lax.slice_in_dim(block, block.shape[dim] - width, None, axis...  28.5 us
    reduce_scatter x1, waiting for transfers between devices, body(): lax.psum_scatter(stacked.astype(jnp.bfloat16), 'phi', scatter_dimension=1...  27.9 us
    ppermute x6, waiting for transfers between devices, with_halo(): lax.ppermute(lax.slice_in_dim(block, 0, width, axis=dim), axis, backward)  19.2 us
    ppermute x6, starting transfers between devices, with_halo(): lax.ppermute(lax.slice_in_dim(block, block.shape[dim] - width, None, axis...  13.3 us
    ppermute x6, starting transfers between devices, with_halo(): lax.ppermute(lax.slice_in_dim(block, 0, width, axis=dim), axis, backward)  8.89 us
    dot_general x2, matrix products, body(): jnp.einsum('bt,tid->bid', messages_onehot, messages_parts, precision=lax....  7.58 us
    dot_general x2, local copies, waits for them, and re-layouts, body(): jnp.einsum('tij,tjd->tid', tile_set, messages_picked, preferred_element_t...  6.92 us
  transfers between devices with their start and end apart: 16, of which 14 were waited for; matrix products, arithmetic and copies ran while one was open for 7% of the time, Pallas kernels for 0%

commit v1 on v0

--- a/solution.py
+++ b/solution.py
@@ -119,7 +119,8 @@
             upstream = live * upstream + back.astype(jnp.float32) + own
     stacked = jnp.stack(partials)
     shares = lax.psum_scatter(stacked.astype(jnp.bfloat16), "phi", scatter_dimension=1, tiled=True)
-    result = lax.psum(shares, ("eta", "half")).astype(jnp.float32)
+    meshes_save = lambda q_in, mesh_name: lax.all_gather(q_in, axis_name=mesh_name).sum(axis=0)
+    result = meshes_save(shares, ("eta", "half")).astype(jnp.float32)
     return (state[None, None], result)
 
 

time: 214 us -> 198 us (0.925)
  waiting for transfers between devices: 113 us -> 96.5 us
    psum x1 -> x0, waiting for transfers between devices: 32.9 us -> none  [body(): result = lax.psum(shares, ('eta', 'half')).astype(jnp.float32)]
    all_gather x0 -> x1, waiting for transfers between devices: none -> 16.9 us  [body(): lax.all_gather(q_in, axis_name=mesh_name).sum(axis=0)]
where the time goes in v1:
time: 198 us; the launch traced here: 197 us
  waiting for transfers between devices  96.5 us (49%)
  local copies, waits for them, and re-layouts  29.8 us (15%)
  matrix products  23.7 us (12%)
  starting transfers between devices  22.3 us (11%)
  between operations  14.9 us (8%)
  other arithmetic  7.9 us (4%)
  blocking collectives  2.35 us (1%)
    ppermute x6, waiting for transfers between devices, with_halo(): lax.ppermute(lax.slice_in_dim(block, block.shape[dim] - width, None, axis...  28.5 us
    reduce_scatter x1, waiting for transfers between devices, body(): lax.psum_scatter(stacked.astype(jnp.bfloat16), 'phi', scatter_dimension=1...  27.9 us
    ppermute x6, waiting for transfers between devices, with_halo(): lax.ppermute(lax.slice_in_dim(block, 0, width, axis=dim), axis, backward)  19.2 us
    all_gather x1, waiting for transfers between devices, body(): lax.all_gather(q_in, axis_name=mesh_name).sum(axis=0)  16.9 us
    ppermute x6, starting transfers between devices, with_halo(): lax.ppermute(lax.slice_in_dim(block, block.shape[dim] - width, None, axis...  13.3 us
    ppermute x6, starting transfers between devices, with_halo(): lax.ppermute(lax.slice_in_dim(block, 0, width, axis=dim), axis, backward)  8.89 us
    dot_general x2, matrix products, body(): jnp.einsum('bt,tid->bid', messages_onehot, messages_parts, precision=lax....  7.58 us
    dot_general x2, local copies, waits for them, and re-layouts, body(): jnp.einsum('tij,tjd->tid', tile_set, messages_picked, preferred_element_t...  6.92 us
  transfers between devices with their start and end apart: 16, of which 14 were waited for; matrix products, arithmetic and copies ran while one was open for 7% of the time, Pallas kernels for 0%

profile of v1, /device:TPU:0, one launch (start us, length us, event | category | flops | bytes accessed | tf_op | source)
XLA Modules:
  0.0 197.5 jit_solution(15014988691890425276)
XLA Ops:
  8.2 3.1 %collective-permute-start = (bf16[1,1,128,512]{3,2,1,0:T(8,128)(2,1)S(1)}, bf16[1,1,128,512]{3,2,1,0:T(8,128)(2,1)S(1)}, u32[]{:S(2)}, u32[]{:S(2)}) collective-permute-start(bf16[1,1,128,512]{3,2,1,0:T(8,128)(2,1)S(1)} %slice.89), channel_id=1, source_target_pairs={{0,4},{4,8},{8,12},{12,0},{1,5},{5,9},{9,13},{13,1},{2,6},{6,10},{... | collective-permute-start | bytes 393224 | tf_op jit(solution)/shard_map/ppermute | solution.py:14
  21.2 10.0 %collective-permute-done.2 = bf16[3,1,128,512]{3,2,1,0:T(8,128)(2,1)S(1)} collective-permute-done((bf16[3,1,128,512]{3,2,1,0:T(8,128)(2,1)S(1)}, bf16[3,1,128,512]{3,2,1,0:T(8,128)(2,1)S(1)}, u32[]{:S(2)}, u32[]{:S(2)}) %collective-permute-start.2) | collective-permute-done | bytes 393248 | tf_op jit(solution)/shard_map/ppermute | solution.py:14
  31.2 6.8 %collective-permute-done.3 = bf16[3,1,128,512]{3,2,1,0:T(8,128)(2,1)S(1)} collective-permute-done((bf16[3,1,128,512]{3,2,1,0:T(8,128)(2,1)S(1)}, bf16[3,1,128,512]{3,2,1,0:T(8,128)(2,1)S(1)}, u32[]{:S(2)}, u32[]{:S(2)}) %collective-permute-start.3) | collective-permute-done | bytes 393248 | tf_op jit(solution)/shard_map/ppermute | solution.py:17
  42.0 3.5 %copy.28 = f32[12,128,512]{2,0,1:T(8,128)} copy(f32[12,128,512]{1,2,0:T(8,128)S(1)} %convolution_bitcast_fusion.2) | data formatting | bytes 6291456 | tf_op jit(solution)/shard_map/tij,tjd->tid/dot_general | solution.py:70
  45.5 3.8 %convolution_convert_fusion.1 = bf16[4,128,512]{2,0,1:T(4,128)(2,1)S(1)} fusion(f32[12,128,512]{2,0,1:T(8,128)} %copy.28, s32[12]{0:T(128)S(1)} %bitcast.120), kind=kOutput, calls=%fused_computation.17 | convolution fusion | flops 38010928 | bytes 3670064 | tf_op jit(solution)/shard_map/bt,tid->bid/dot_general | solution.py:74
  50.3 2.3 %broadcast_in_dim.41 = f32[2,8,64,8,64]{4,3,2,1,0:T(8,128)} broadcast(f32[2,8,8]{2,1,0:T(8,128)S(1)} %convert_element_type.117), dimensions={0,1,3} | broadcast | bytes 2097664 | tf_op jit(solution)/shard_map/broadcast_in_dim | solution.py:49
  52.6 3.5 %convert_element_type.118 = f32[2,512,512]{2,1,0:T(8,128)S(1)} reshape(f32[2,8,64,8,64]{4,3,2,1,0:T(8,128)} %broadcast_in_dim.41) | data formatting | bytes 4194304 | tf_op jit(solution)/shard_map/convert_element_type | solution.py:51
  58.7 2.4 %fusion.20 = (bf16[256,512]{1,0:T(8,128)(2,1)S(1)}, f32[256,512]{1,0:T(8,128)}) fusion(bf16[1,1,256,512]{3,2,1,0:T(8,128)(2,1)} %param.10, f32[256]{0:T(256)} %compare_convert_fusion.1, bf16[2,512,512]{2,1,0:T(8,128)(2,1)} %multiply_convert_fusion, bf16[256,512]{1,0:T(8,128)(2,1)} %reduce-scatter.4.cloned.1.call-done), kind=kOutput, calls=%fused_computation.37 | convolution fusion | flops 135790592 | bytes 2098176 | tf_op jit(solution)/shard_map/dot_general | solution.py:83
  65.0 4.4 %collective-permute-done.4 = bf16[1,1,128,512]{3,2,1,0:T(8,128)(2,1)S(1)} collective-permute-done((bf16[1,1,128,512]{3,2,1,0:T(8,128)(2,1)S(1)}, bf16[1,1,128,512]{3,2,1,0:T(8,128)(2,1)S(1)}, u32[]{:S(2)}, u32[]{:S(2)}) %collective-permute-start.4) | collective-permute-done | bytes 131104 | tf_op jit(solution)/shard_map/ppermute | solution.py:14
  72.6 10.0 %collective-permute-done.6 = bf16[3,1,128,512]{3,2,1,0:T(8,128)(2,1)S(1)} collective-permute-done((bf16[3,1,128,512]{3,2,1,0:T(8,128)(2,1)S(1)}, bf16[3,1,128,512]{3,2,1,0:T(8,128)(2,1)S(1)}, u32[]{:S(2)}, u32[]{:S(2)}) %collective-permute-start.6) | collective-permute-done | bytes 393248 | tf_op jit(solution)/shard_map/ppermute | solution.py:14
  82.7 6.9 %collective-permute-done.7 = bf16[3,1,128,512]{3,2,1,0:T(8,128)(2,1)S(1)} collective-permute-done((bf16[3,1,128,512]{3,2,1,0:T(8,128)(2,1)S(1)}, bf16[3,1,128,512]{3,2,1,0:T(8,128)(2,1)S(1)}, u32[]{:S(2)}, u32[]{:S(2)}) %collective-permute-start.7) | collective-permute-done | bytes 393248 | tf_op jit(solution)/shard_map/ppermute | solution.py:17
  93.6 3.5 %copy.31 = f32[12,128,512]{2,0,1:T(8,128)} copy(f32[12,128,512]{1,2,0:T(8,128)S(1)} %convolution_bitcast_fusion.1) | data formatting | bytes 6291456 | tf_op jit(solution)/shard_map/tij,tjd->tid/dot_general | solution.py:70
  97.1 3.8 %convolution_convert_fusion = bf16[4,128,512]{2,0,1:T(4,128)(2,1)S(1)} fusion(f32[12,128,512]{2,0,1:T(8,128)} %copy.31, s32[12]{0:T(128)S(1)} %bitcast.121), kind=kOutput, calls=%fused_computation.16 | convolution fusion | flops 38010928 | bytes 3670064 | tf_op jit(solution)/shard_map/bt,tid->bid/dot_general | solution.py:74
  105.3 4.0 %reduce-scatter.6.cloned.1.call-done = bf16[256,512]{1,0:T(8,128)(2,1)} async-done(((bf16[512,512]{1,0:T(8,128)(2,1)}), bf16[256,512]{1,0:T(8,128)(2,1)}) %reduce-scatter.6.cloned.1.call-update) | async-done | bytes 262160 | tf_op jit(solution)/shard_map/reduce_scatter | solution.py:78
  109.3 2.4 %fusion.27 = (bf16[256,512]{1,0:T(8,128)(2,1)S(1)}, bf16[1,1,256,512]{3,2,1,0:T(8,128)(2,1)}) fusion(bf16[1,1,256,512]{3,2,1,0:T(8,128)(2,1)S(1)} %copy-done.19, f32[256]{0:T(256)S(1)} %copy-done.17, bf16[256,512]{1,0:T(8,128)(2,1)S(1)} %copy-done.3, bf16[2,512,512]{2,1,0:T(8,128)(2,1)} %multiply_convert_fusion, ...), kind=kOutput, calls=%fused_computation.48 | convolution fusion | flops 136839168 | bytes 2098176 | tf_op jit(solution)/shard_map/dot_general | solution.py:83
  112.7 2.3 %all_gather.9 = bf16[512,512]{1,0:T(8,128)(2,1)S(1)} all-gather(bf16[256,512]{1,0:T(8,128)(2,1)S(1)} %convolution_convert_fusion.2), channel_id=1, replica_groups=mesh['group'=2,'phi'=4,'eta'=2,'half'=2] {'half'}, dimensions={0}, use_global_device_ids=true | all-gather | bytes 786432 | tf_op jit(solution)/shard_map/all_gather | solution.py:99
  116.9 2.1 %convolution_bitcast_fusion = f32[12,128,512]{1,2,0:T(8,128)S(1)} fusion(bf16[12,128,512]{2,1,0:T(8,128)(2,1)} %gather_fusion, pred[12]{0:T(512)(128)(4,1)S(1)} %get-tuple-element.18, bf16[12]{0:T(256)(128)(2,1)S(1)} %get-tuple-element.17, bf16[1,1,12,128,128]{4,3,2,1,0:T(8,128)(2,1)S(1)} %copy-done), kind=kOutput, calls=%fused_computation.4 | convolution fusion | flops 202899456 | bytes 5111844 | tf_op jit(solution)/shard_map/tji,tjd->tid/dot_general | solution.py:107
  119.1 3.5 %copy.34 = f32[12,128,512]{2,0,1:T(8,128)} copy(f32[12,128,512]{1,2,0:T(8,128)S(1)} %convolution_bitcast_fusion) | data formatting | bytes 6291456 | tf_op jit(solution)/shard_map/tji,tjd->tid/dot_general | solution.py:107
  122.6 3.7 %fusion.53 = f32[6,128,512]{2,0,1:T(8,128)S(1)} fusion(f32[12,128,512]{2,0,1:T(8,128)} %copy.34, s32[12]{0:T(128)S(1)} %bitcast.122), kind=kOutput, calls=%fused_computation.96 | convolution fusion | flops 56623176 | bytes 4718640 | tf_op jit(solution)/shard_map/st,tid->sid/dot_general | solution.py:109
  127.4 3.8 %collective-permute-start.10 = (bf16[1,128,512]{2,1,0:T(8,128)(2,1)S(1)}, bf16[1,128,512]{2,1,0:T(8,128)(2,1)S(1)}, u32[]{:S(2)}, u32[]{:S(2)}) collective-permute-start(bf16[1,128,512]{2,1,0:T(8,128)(2,1)S(1)} %get-tuple-element.9), channel_id=1, source_target_pairs={{0,2},{1,3},{4,6},{5,7},{8,10},{9,11},{12,14},{13,15},{16,18},{17,... | collective-permute-start | bytes 393224 | tf_op jit(solution)/shard_map/ppermute | solution.py:14
  134.0 2.3 %collective-permute-start.9 = (bf16[1,128,512]{2,1,0:T(8,128)(2,1)S(1)}, bf16[1,128,512]{2,1,0:T(8,128)(2,1)S(1)}, u32[]{:S(2)}, u32[]{:S(2)}) collective-permute-start(bf16[1,128,512]{2,1,0:T(8,128)(2,1)S(1)} %get-tuple-element.10), channel_id=1, source_target_pairs={{4,0},{8,4},{12,8},{0,12},{5,1},{9,5},{13,9},{1,13},{6,2},{10,6},{... | collective-permute-start | bytes 393224 | tf_op jit(solution)/shard_map/ppermute | solution.py:17
  138.5 2.2 %collective-permute-done.8 = bf16[1,128,512]{2,1,0:T(8,128)(2,1)S(1)} collective-permute-done((bf16[1,128,512]{2,1,0:T(8,128)(2,1)S(1)}, bf16[1,128,512]{2,1,0:T(8,128)(2,1)S(1)}, u32[]{:S(2)}, u32[]{:S(2)}) %collective-permute-start.8) | collective-permute-done | bytes 131104 | tf_op jit(solution)/shard_map/ppermute | solution.py:14
  143.9 27.9 %reduce-scatter.8.cloned.1.call-done = bf16[2,128,512]{2,1,0:T(8,128)(2,1)} async-done(((bf16[2,512,512]{2,1,0:T(8,128)(2,1)}), bf16[2,128,512]{2,1,0:T(8,128)(2,1)}) %reduce-scatter.8.cloned.1.call-update) | async-done | bytes 262160 | tf_op jit(solution)/shard_map/reduce_scatter | solution.py:121
  171.8 16.9 %all-gather.3.cloned.1.call-done = bf16[8,128,512]{2,1,0:T(8,128)(2,1)} async-done(((bf16[2,128,512]{2,1,0:T(8,128)(2,1)}), bf16[8,128,512]{2,1,0:T(8,128)(2,1)}) %all-gather.3.cloned.1.call-update) | async-done | bytes 1048592 | tf_op jit(solution)/shard_map/all_gather | solution.py:122
  (115 shorter events, 47.7 us)
Async XLA Ops:
  7.2 32.7 %copy-start = (bf16[1,1,12,128,128]{4,3,2,1,0:T(8,128)(2,1)S(1)}, bf16[1,1,12,128,128]{4,3,2,1,0:T(8,128)(2,1)}, u32[]{:S(2)}) copy-start(bf16[1,1,12,128,128]{4,3,2,1,0:T(8,128)(2,1)} %param.12) | copy-start | bytes 1179652
  7.2 51.5 %reduce-scatter.4.cloned.1.call-start = ((), (), s32[]{:S(2)}) async-start(), calls=%async_computation.3 | async-start | bytes 786432 | tf_op jit(solution)/shard_map/reduce_scatter | solution.py:78
  8.2 9.4 %collective-permute-start = (bf16[1,1,128,512]{3,2,1,0:T(8,128)(2,1)S(1)}, bf16[1,1,128,512]{3,2,1,0:T(8,128)(2,1)S(1)}, u32[]{:S(2)}, u32[]{:S(2)}) collective-permute-start(bf16[1,1,128,512]{3,2,1,0:T(8,128)(2,1)S(1)} %slice.89), channel_id=1, source_target_pairs={{0,4},{4,8},{8,12},{12,0},{1,5},{5,9},{9,13},{13,1},{2,6},{6,10},{... | collective-permute-start | bytes 393224 | tf_op jit(solution)/shard_map/ppermute | solution.py:14
  11.3 7.8 %collective-permute-start.1 = (bf16[1,1,128,512]{3,2,1,0:T(8,128)(2,1)S(1)}, bf16[1,1,128,512]{3,2,1,0:T(8,128)(2,1)S(1)}, u32[]{:S(2)}, u32[]{:S(2)}) collective-permute-start(bf16[1,1,128,512]{3,2,1,0:T(8,128)(2,1)S(1)} %slice.89), channel_id=1, source_target_pairs={{4,0},{8,4},{12,8},{0,12},{5,1},{9,5},{13,9},{1,13},{6,2},{10,6},{... | collective-permute-start | bytes 393224 | tf_op jit(solution)/shard_map/ppermute | solution.py:17
  14.7 25.2 %copy-start.16 = (pred[12]{0:T(512)(128)(4,1)}, pred[12]{0:T(512)(128)(4,1)S(1)}, u32[]{:S(2)}) copy-start(pred[12]{0:T(512)(128)(4,1)S(1)} %compare_and_fusion) | copy-start | bytes 40
  19.1 12.1 %collective-permute-start.2 = (bf16[3,1,128,512]{3,2,1,0:T(8,128)(2,1)S(1)}, bf16[3,1,128,512]{3,2,1,0:T(8,128)(2,1)S(1)}, u32[]{:S(2)}, u32[]{:S(2)}) collective-permute-start(bf16[3,1,128,512]{3,2,1,0:T(8,128)(2,1)S(1)} %pad_maximum_fusion.1), channel_id=1, source_target_pairs={{0,2},{2,0},{1,3},{3,1},{4,6},{6,4},{5,7},{7,5},{8,10},{10,8},{9,1... | collective-permute-start | bytes 1179656 | tf_op jit(solution)/shard_map/ppermute | solution.py:14
  20.6 17.4 %collective-permute-start.3 = (bf16[3,1,128,512]{3,2,1,0:T(8,128)(2,1)S(1)}, bf16[3,1,128,512]{3,2,1,0:T(8,128)(2,1)S(1)}, u32[]{:S(2)}, u32[]{:S(2)}) collective-permute-start(bf16[3,1,128,512]{3,2,1,0:T(8,128)(2,1)S(1)} %pad_maximum_fusion.1), channel_id=1, source_target_pairs={{2,0},{0,2},{3,1},{1,3},{6,4},{4,6},{7,5},{5,7},{10,8},{8,10},{11,... | collective-permute-start | bytes 1179656 | tf_op jit(solution)/shard_map/ppermute | solution.py:17
  50.2 59.1 %reduce-scatter.6.cloned.1.call-start = ((), (), s32[]{:S(2)}) async-start(), calls=%async_computation.4 | async-start | bytes 786432 | tf_op jit(solution)/shard_map/reduce_scatter | solution.py:78
  61.1 21.6 %copy-start.2 = (bf16[256,512]{1,0:T(8,128)(2,1)}, bf16[256,512]{1,0:T(8,128)(2,1)S(1)}, u32[]{:S(2)}) copy-start(bf16[256,512]{1,0:T(8,128)(2,1)S(1)} %get-tuple-element.19) | copy-start | bytes 786436
  61.1 8.3 %collective-permute-start.4 = (bf16[1,1,128,512]{3,2,1,0:T(8,128)(2,1)S(1)}, bf16[1,1,128,512]{3,2,1,0:T(8,128)(2,1)S(1)}, u32[]{:S(2)}, u32[]{:S(2)}) collective-permute-start(bf16[1,1,128,512]{3,2,1,0:T(8,128)(2,1)S(1)} %slice_bitcast_fusion.6), channel_id=1, source_target_pairs={{0,4},{4,8},{8,12},{12,0},{1,5},{5,9},{9,13},{13,1},{2,6},{6,10},{... | collective-permute-start | bytes 393224 | tf_op jit(solution)/shard_map/ppermute | solution.py:14
  62.9 7.6 %collective-permute-start.5 = (bf16[1,1,128,512]{3,2,1,0:T(8,128)(2,1)S(1)}, bf16[1,1,128,512]{3,2,1,0:T(8,128)(2,1)S(1)}, u32[]{:S(2)}, u32[]{:S(2)}) collective-permute-start(bf16[1,1,128,512]{3,2,1,0:T(8,128)(2,1)S(1)} %slice_bitcast_fusion.6), channel_id=1, source_target_pairs={{4,0},{8,4},{12,8},{0,12},{5,1},{9,5},{13,9},{1,13},{6,2},{10,6},{... | collective-permute-start | bytes 393224 | tf_op jit(solution)/shard_map/ppermute | solution.py:17
  70.5 12.1 %collective-permute-start.6 = (bf16[3,1,128,512]{3,2,1,0:T(8,128)(2,1)S(1)}, bf16[3,1,128,512]{3,2,1,0:T(8,128)(2,1)S(1)}, u32[]{:S(2)}, u32[]{:S(2)}) collective-permute-start(bf16[3,1,128,512]{3,2,1,0:T(8,128)(2,1)S(1)} %pad_maximum_fusion.2), channel_id=1, source_target_pairs={{0,2},{2,0},{1,3},{3,1},{4,6},{6,4},{5,7},{7,5},{8,10},{10,8},{9,1... | collective-permute-start | bytes 1179656 | tf_op jit(solution)/shard_map/ppermute | solution.py:14
  72.0 17.5 %collective-permute-start.7 = (bf16[3,1,128,512]{3,2,1,0:T(8,128)(2,1)S(1)}, bf16[3,1,128,512]{3,2,1,0:T(8,128)(2,1)S(1)}, u32[]{:S(2)}, u32[]{:S(2)}) collective-permute-start(bf16[3,1,128,512]{3,2,1,0:T(8,128)(2,1)S(1)} %pad_maximum_fusion.2), channel_id=1, source_target_pairs={{2,0},{0,2},{3,1},{1,3},{6,4},{4,6},{7,5},{5,7},{10,8},{8,10},{11,... | collective-permute-start | bytes 1179656 | tf_op jit(solution)/shard_map/ppermute | solution.py:17
  101.8 70.0 %reduce-scatter.8.cloned.1.call-start = ((), (), s32[]{:S(2)}) async-start(), calls=%async_computation.5 | async-start | bytes 1310720 | tf_op jit(solution)/shard_map/reduce_scatter | solution.py:121
  105.2 6.4 %copy-start.7 = (bf16[2,512,512]{2,1,0:T(8,128)(2,1)S(1)}, bf16[2,512,512]{2,1,0:T(8,128)(2,1)}, u32[]{:S(2)}) copy-start(bf16[2,512,512]{2,1,0:T(8,128)(2,1)} %multiply_convert_fusion) | copy-start | bytes 3145732
  127.3 9.1 %copy-start.1 = (f32[512,512]{1,0:T(8,128)S(1)}, f32[512,512]{1,0:T(8,128)}, u32[]{:S(2)}) copy-start(f32[512,512]{1,0:T(8,128)} %squeeze.39) | copy-start | bytes 3145732
  127.3 9.1 %copy-start.4 = (bf16[256,512]{1,0:T(8,128)(2,1)S(1)}, bf16[256,512]{1,0:T(8,128)(2,1)}, u32[]{:S(2)}) copy-start(bf16[256,512]{1,0:T(8,128)(2,1)} %copy-done.2) | copy-start | bytes 786436
  127.3 9.1 %copy-start.11 = (bf16[256,512]{1,0:T(8,128)(2,1)S(1)}, bf16[256,512]{1,0:T(8,128)(2,1)}, u32[]{:S(2)}) copy-start(bf16[256,512]{1,0:T(8,128)(2,1)} %reduce-scatter.6.cloned.1.call-done) | copy-start | bytes 786436
  127.3 9.0 %copy-start.13 = (bf16[256,512]{1,0:T(8,128)(2,1)S(1)}, bf16[256,512]{1,0:T(8,128)(2,1)}, u32[]{:S(2)}) copy-start(bf16[256,512]{1,0:T(8,128)(2,1)} %copy-done.12) | copy-start | bytes 786436
  127.4 9.4 %collective-permute-start.10 = (bf16[1,128,512]{2,1,0:T(8,128)(2,1)S(1)}, bf16[1,128,512]{2,1,0:T(8,128)(2,1)S(1)}, u32[]{:S(2)}, u32[]{:S(2)}) collective-permute-start(bf16[1,128,512]{2,1,0:T(8,128)(2,1)S(1)} %get-tuple-element.9), channel_id=1, source_target_pairs={{0,2},{1,3},{4,6},{5,7},{8,10},{9,11},{12,14},{13,15},{16,18},{17,... | collective-permute-start | bytes 393224 | tf_op jit(solution)/shard_map/ppermute | solution.py:14
  131.1 7.3 %collective-permute-start.11 = (bf16[1,128,512]{2,1,0:T(8,128)(2,1)S(1)}, bf16[1,128,512]{2,1,0:T(8,128)(2,1)S(1)}, u32[]{:S(2)}, u32[]{:S(2)}) collective-permute-start(bf16[1,128,512]{2,1,0:T(8,128)(2,1)S(1)} %get-tuple-element.8), channel_id=1, source_target_pairs={{2,0},{3,1},{6,4},{7,5},{10,8},{11,9},{14,12},{15,13},{18,16},{19,... | collective-permute-start | bytes 393224 | tf_op jit(solution)/shard_map/ppermute | solution.py:17
  132.4 8.2 %collective-permute-start.8 = (bf16[1,128,512]{2,1,0:T(8,128)(2,1)S(1)}, bf16[1,128,512]{2,1,0:T(8,128)(2,1)S(1)}, u32[]{:S(2)}, u32[]{:S(2)}) collective-permute-start(bf16[1,128,512]{2,1,0:T(8,128)(2,1)S(1)} %get-tuple-element.7), channel_id=1, source_target_pairs={{0,4},{4,8},{8,12},{12,0},{1,5},{5,9},{9,13},{13,1},{2,6},{6,10},{... | collective-permute-start | bytes 393224 | tf_op jit(solution)/shard_map/ppermute | solution.py:14
  134.0 8.0 %collective-permute-start.9 = (bf16[1,128,512]{2,1,0:T(8,128)(2,1)S(1)}, bf16[1,128,512]{2,1,0:T(8,128)(2,1)S(1)}, u32[]{:S(2)}, u32[]{:S(2)}) collective-permute-start(bf16[1,128,512]{2,1,0:T(8,128)(2,1)S(1)} %get-tuple-element.10), channel_id=1, source_target_pairs={{4,0},{8,4},{12,8},{0,12},{5,1},{9,5},{13,9},{1,13},{6,2},{10,6},{... | collective-permute-start | bytes 393224 | tf_op jit(solution)/shard_map/ppermute | solution.py:17
  143.8 44.8 %all-gather.3.cloned.1.call-start = ((), (), s32[]{:S(2)}) async-start(), calls=%async_computation.6 | async-start | bytes 1310720 | tf_op jit(solution)/shard_map/all_gather | solution.py:122
  (15 other events, 68.0 us)
Sparse Core Ops, SparseCore 0:
  50.3 7.6 reduce-scatter.3
  101.9 7.3 reduce-scatter.5
  143.9 27.7 reduce-scatter.7
  173.2 15.3 all-gather.2
